TPU v7x, 32 devices: a whole 2x2x4 slice. The times are simulated.
32 devices in a mesh: groups: 2 (over y), row: 16 (over z, x, core).
Axes of the slice: x: 2, y: 2, z: 4, core: 2. Of those that a mesh axis runs over, the one named last changes fastest.
Arguments:
- late_grads: bfloat16 [64, 16, 4, 4096], P(('groups', 'row')), parts along dimension 0, may hold values from -6 to 6
- projections: bfloat16 [4096, 256], replicated, may hold values from -0.09375 to 0.09375
- recent_sketches: bfloat16 [8192, 8192], P(('groups', 'row')), parts along dimension 0, may hold values from -6 to 6
Outputs:
- reweighted: bfloat16 [64, 8192], P(('groups', 'row')), parts along dimension 0
There are 2 independent parts, one for each index of `groups`. A program takes and returns all parts, laid end to end along the dimension named above; an argument that names none is the same for every part. Nothing has to cross between parts.
All inputs are finite; a program needn't handle non-finite values.
Results may differ from a plain program's by a relative error of at most 0.0076.
Values may be sent and summed in bfloat16 or wider, within the bound.
A program may use at most 64 MiB of HBM per device.

v0:
```python
import jax
import jax.numpy as jnp
from jax import lax
from jax.sharding import PartitionSpec as P


def build_sketch(factors, items, rank):
    count = factors.shape[0]
    parts = factors.reshape(count, items, 4, rank)
    blocks = []
    for layer in range(2):
        outer = jnp.einsum(
            "eti,etj->eij",
            parts[:, :, 2 * layer + 1, :],
            parts[:, :, 2 * layer, :],
            preferred_element_type=jnp.float32,
        )
        blocks.append(outer.reshape(count, rank * rank))
    joined = jnp.concatenate(blocks, axis=1) / jnp.sqrt(jnp.float32(items))
    return joined.astype(jnp.bfloat16)


def weighted_term(late_rows, recent_sketches, width):
    similarity = jnp.dot(
        late_rows, recent_sketches.T, preferred_element_type=jnp.float32
    ) / jnp.sqrt(jnp.float32(width))
    weights = jnp.tanh(similarity).astype(jnp.bfloat16)
    return jnp.dot(weights, recent_sketches, preferred_element_type=jnp.float32)


def per_device(late_grads, projections, recent_sketches):
    local_rows, items, kinds, width_in = late_grads.shape
    rank = projections.shape[1] // 4
    width = recent_sketches.shape[1]
    total_recent = recent_sketches.shape[0] * lax.axis_size("row")
    proj_blocks = projections.reshape(width_in, 4, rank)
    factors = jnp.einsum(
        "etkd,dkr->etkr", late_grads, proj_blocks, preferred_element_type=jnp.float32
    )
    factors = factors.astype(jnp.bfloat16).reshape(local_rows, items, 4 * rank)
    own_sketch = build_sketch(factors, items, rank)
    late_all = lax.all_gather(own_sketch, "row", axis=0, tiled=True)
    scale = jnp.sqrt(jnp.float32(total_recent))
    term = weighted_term(late_all, recent_sketches, width)
    col_block = lax.psum_scatter(term, "row", scatter_dimension=1, tiled=True)
    finished = (col_block / scale).astype(jnp.bfloat16)
    result = lax.all_to_all(finished, "row", split_axis=0, concat_axis=1, tiled=True)
    return result


def solution(mesh):
    placed = (P(("groups", "row"), None, None, None), P(), P(("groups", "row"), None))
    return jax.shard_map(
        per_device,
        mesh=mesh,
        in_specs=placed,
        out_specs=P(("groups", "row"), None),
        check_vma=False,
    )
```

profile of v0, /device:TPU:0, one launch (start us, length us, event | category | flops | bytes accessed | tf_op | source)
XLA Modules:
  0.0 118.1 jit_solution(12450617553153729019)
XLA Ops:
  6.5 0.0 reduce-scatter.2.cloned.1.call-start
  6.5 1.8 %copy.11 = bf16[2,16,4,4096]{3,1,0,2:T(8,128)(2,1)S(1)} copy(bf16[2,16,4,4096]{3,2,1,0:T(4,128)(2,1)} %param.3) | data formatting | bytes 2097152 | tf_op args[0]
  8.3 2.9 %copy.10 = bf16[4096,256]{0,1:T(8,128)(2,1)S(1)} copy(bf16[4096,256]{1,0:T(8,128)(2,1)} %param.4) | data formatting | bytes 4194304 | tf_op args[1]
  11.3 0.7 fusion.9
  12.0 0.2 fusion.7
  12.2 0.2 fusion.6
  12.4 0.1 reshape.13
  12.5 0.1 reshape.14
  12.6 24.6 %all-gather = bf16[16,2,8192]{2,1,0:T(2,128)(2,1)S(1)} all-gather(bf16[1,2,8192]{2,1,0:T(2,128)(2,1)S(1)} %fusion.4), channel_id=1, replica_groups=mesh['groups'=2,'row'=16] {'row'}, dimensions={0}, use_global_device_ids=true | all-gather | bytes 557056 | tf_op jit(solution)/shard_map/all_gather | solution.py:42
  37.2 0.2 reshape.16
  37.4 7.4 %fusion.2 = f32[32,8192]{1,0:T(8,128)} fusion(bf16[256,8192]{1,0:T(8,128)(2,1)} %param.5, bf16[32,8192]{1,0:T(8,128)(2,1)S(1)} %reshape.16), kind=kOutput, calls=%fused_computation.3 | convolution fusion | flops 268451840 | bytes 5767168 | tf_op jit(solution)/shard_map/dot_general | solution.py:28
  44.8 0.0 reduce-scatter.2.cloned.1.call-update
  44.8 54.8 %reduce-scatter.2.cloned.1.call-done = f32[32,512]{1,0:T(8,128)} async-done(((f32[32,8192]{1,0:T(8,128)}), f32[32,512]{1,0:T(8,128)}) %reduce-scatter.2.cloned.1.call-update) | async-done | bytes 65552 | tf_op jit(solution)/shard_map/reduce_scatter | solution.py:45
  99.6 0.8 multiply_convert_fusion
  100.4 10.2 %all_to_all.19 = bf16[16,2,512]{2,1,0:T(2,128)(2,1)S(1)} all-to-all(bf16[16,2,512]{2,1,0:T(2,128)(2,1)S(1)} %all_to_all.14), channel_id=1, replica_groups=mesh['groups'=2,'row'=16] {'row'}, dimensions={0} | all-to-all | bytes 65536 | tf_op jit(solution)/shard_map/all_to_all | solution.py:47
  110.6 0.6 copy.14
  (3 shorter events, 0.1 us)
Async XLA Ops:
  6.5 93.0 %reduce-scatter.2.cloned.1.call-start = ((), (), s32[]{:S(2)}) async-start(), calls=%async_computation.2 | async-start | bytes 1114112 | tf_op jit(solution)/shard_map/reduce_scatter | solution.py:45
Sparse Core Ops, SparseCore 0:
  44.9 54.6 reduce-scatter.1
where the time goes:
time: 118 us
  waiting for transfers between devices  54.8 us (46%)
  blocking collectives  34.8 us (29%)
  between operations  13.4 us (11%)
  matrix products  8.43 us (7%)
  local copies, waits for them, and re-layouts  5.74 us (5%)
    reduce_scatter x1, waiting for transfers between devices, per_device(): col_block = lax.psum_scatter(term, 'row', scatter_dimension=1, tiled=True)  54.8 us
    all_gather x1, blocking collectives, per_device(): late_all = lax.all_gather(own_sketch, 'row', axis=0, tiled=True)  24.6 us
    all_to_all x1, blocking collectives, per_device(): lax.all_to_all(finished, 'row', split_axis=0, concat_axis=1, tiled=True)  10.2 us
    dot_general x1, matrix products, weighted_term(): return jnp.dot(weights, recent_sketches, preferred_element_type=jnp.float32)  7.37 us
    unnamed x4, local copies, waits for them, and re-layouts  5.53 us
  transfers between devices with their start and end apart: 1, of which 1 were waited for; matrix products, arithmetic and copies ran while one was open for 0% of the time, Pallas kernels for 0%

commit v1 on v0

v1 whole, which is shorter than its diff:
```python
import functools
import math

import jax
import jax.numpy as jnp
from jax import lax
from jax.experimental import pallas as pl
from jax.experimental.pallas import tpu as pltpu
from jax.sharding import PartitionSpec as P

GROUP = 8
CHUNKS = 4
MESH = pl.DeviceIdType.MESH


def kernel(
    dims, items, rank, total_recent,
    late_hbm, proj_hbm, recent_hbm, out_ref,
    late, proj, recent, gath, wmask, tf, tb, r1, s1f, s1b, r2, s2f, s2b, r3,
    load_sem, g_send, g_recv, c_send, c_recv, x_send, x_recv, z_send, z_recv,
):
    nz, nx, nc = dims
    width = recent_hbm.shape[1]
    part = width // GROUP
    local_recent = recent_hbm.shape[0]
    slab = gath.shape[3]
    examples = slab // GROUP
    n = nz * nx * nc
    me = lax.axis_index("row")
    mc = lax.rem(me, nc)
    mx = lax.rem(lax.div(me, nc), nx)
    mz = lax.div(me, nc * nx)
    oc = 1 - mc

    def flat(z, x, c):
        return {"row": (z * nx + x) * nc + c}

    load_late = pltpu.make_async_copy(late_hbm, late, load_sem.at[0])
    load_proj = pltpu.make_async_copy(proj_hbm, proj, load_sem.at[1])
    load_late.start()
    load_proj.start()
    load_recent = []
    for q in range(GROUP):
        copy = pltpu.make_async_copy(
            recent_hbm.at[:, pl.ds(q * part, part)],
            recent.at[pl.ds(q * local_recent, local_recent), :],
            load_sem.at[2 + q],
        )
        copy.start()
        load_recent.append(copy)

    peers = [(mz, mx, oc)]
    peers += [(mz, lax.rem(mx + d, nx), mc) for d in range(1, nx)]
    peers += [(lax.rem(mz + d, nz), mx, mc) for d in range(1, nz)]
    barrier = pltpu.get_barrier_semaphore()
    for z, x, c in peers:
        pl.semaphore_signal(barrier, inc=1, device_id=flat(z, x, c), device_id_type=MESH)

    def onehot(shape, expr):
        r = lax.broadcasted_iota(jnp.int32, shape, 0)
        c = lax.broadcasted_iota(jnp.int32, shape, 1)
        return jnp.where(expr(r, c), 1.0, 0.0).astype(jnp.bfloat16)

    pairs = examples * items
    pick = onehot((pairs, 4 * pairs), lambda r, c: r == lax.shift_right_logical(c, 2))
    spread = onehot((rank, part), lambda r, c: r == lax.rem(c, rank))
    repeat = onehot((rank, rank * rank), lambda r, c: r == lax.div(c, rank))

    load_late.wait()
    load_proj.wait()
    rows = late[...].reshape(4 * pairs, late.shape[2])
    full = jnp.dot(rows, proj[...], preferred_element_type=jnp.float32)
    kind = lax.rem(lax.broadcasted_iota(jnp.int32, full.shape, 0), 4)
    block = lax.div(lax.broadcasted_iota(jnp.int32, full.shape, 1), rank)
    full = jnp.where(kind == block, full, 0.0).astype(jnp.bfloat16)
    factors = jnp.dot(pick, full, preferred_element_type=jnp.float32)
    sketch = jnp.zeros((slab, part), jnp.float32)
    row = lax.broadcasted_iota(jnp.int32, (slab, part), 0)
    quarter = GROUP // 2
    for layer in range(2):
        right = factors[:, 2 * layer * rank : (2 * layer + 1) * rank].astype(jnp.bfloat16)
        left = factors[:, (2 * layer + 1) * rank : (2 * layer + 2) * rank].astype(jnp.bfloat16)
        tiled = jnp.dot(right, spread, preferred_element_type=jnp.float32)
        for q in range(quarter):
            wide = jnp.dot(
                left, repeat[:, q * part : (q + 1) * part], preferred_element_type=jnp.float32
            )
            outer = wide * tiled
            for e in range(examples):
                total = jnp.sum(outer[e * items : (e + 1) * items], axis=0, keepdims=True)
                at = e * GROUP + layer * quarter + q
                sketch = jnp.where(row == at, total, sketch)
    gath[mz, mx, mc] = (sketch * (1.0 / math.sqrt(items))).astype(jnp.bfloat16)

    pl.semaphore_wait(barrier, len(peers))

    sent = []

    def forward(z, x, c, to, slot):
        copy = pltpu.make_async_remote_copy(
            src_ref=gath.at[z, x, c], dst_ref=gath.at[z, x, c],
            send_sem=g_send.at[slot], recv_sem=g_recv.at[z, x, c],
            device_id=flat(*to), device_id_type=MESH,
        )
        copy.start()
        sent.append(copy)

    def arrived(z, x, c):
        pltpu.make_async_remote_copy(
            src_ref=gath.at[z, x, c], dst_ref=gath.at[z, x, c],
            send_sem=g_send.at[0], recv_sem=g_recv.at[z, x, c],
            device_id=flat(mz, mx, oc), device_id_type=MESH,
        ).wait_recv()

    slot = 0
    for d in range(1, nz):
        forward(mz, mx, mc, (lax.rem(mz + d, nz), mx, mc), slot)
        slot += 1
    for dz in range(nz):
        z = lax.rem(mz + nz - dz, nz)
        if dz:
            arrived(z, mx, mc)
        for d in range(1, nx):
            forward(z, mx, mc, (mz, lax.rem(mx + d, nx), mc), slot)
            slot += 1
        forward(z, mx, mc, (mz, mx, oc), slot)
        slot += 1
    for dz in range(nz):
        z = lax.rem(mz + nz - dz, nz)
        for d in range(1, nx):
            x = lax.rem(mx + nx - d, nx)
            arrived(z, x, mc)
            forward(z, x, mc, (mz, mx, oc), slot)
            slot += 1
    for copy in load_recent:
        copy.wait()
    for dz in range(nz):
        z = lax.rem(mz + nz - dz, nz)
        for d in range(nx):
            arrived(z, lax.rem(mx + nx - d, nx), oc)

    zb = max(1, min(nz, 256 // (nx * nc * slab)))
    rb = zb * nx * nc * slab

    def similar(b):
        base = b * zb
        every = gath[pl.ds(base, zb)].reshape(rb, part)
        group = lax.rem(lax.broadcasted_iota(jnp.int32, (rb, local_recent), 0), GROUP)
        acc = jnp.zeros((rb, local_recent), jnp.float32)
        for q in range(GROUP):
            term = lax.dot_general(
                every, recent[q * local_recent : (q + 1) * local_recent, :],
                (((1,), (1,)), ((), ())), preferred_element_type=jnp.float32,
            )
            acc = jnp.where(group == q, term, acc)
        acc = acc.reshape(rb // GROUP, GROUP, local_recent)
        sim = jnp.sum(acc, axis=1, keepdims=True) * (1.0 / math.sqrt(width))
        weights = jnp.broadcast_to(jnp.tanh(sim), acc.shape).reshape(rb, local_recent)
        for q in range(GROUP):
            wmask[pl.ds(b * rb, rb), q * local_recent : (q + 1) * local_recent] = jnp.where(
                group == q, weights, 0.0
            ).astype(jnp.bfloat16)

    def each_block(body):
        if nz == zb:
            body(0)
        else:
            lax.fori_loop(0, nz // zb, lambda b, c: (body(b), c)[1], 0)

    each_block(similar)

    cw = part // CHUNKS
    copies = []

    def start(src, dst, ss, rs, to):
        copy = pltpu.make_async_remote_copy(
            src_ref=src, dst_ref=dst, send_sem=ss, recv_sem=rs,
            device_id=flat(*to), device_id_type=MESH,
        )
        copy.start()
        copies.append(copy)
        return copy

    core_copies, x_copies, z_copies = {}, {}, {}

    def stage_core(k):
        cols = pl.ds(k * cw, cw)

        def body(b):
            term = jnp.dot(
                wmask[pl.ds(b * rb, rb), :], recent[:, k * cw : (k + 1) * cw],
                preferred_element_type=jnp.float32,
            ).reshape(zb, nx, nc, slab, cw)
            tf[pl.ds(b * zb, zb), :, :, :, cols] = term
            tb[pl.ds(b * zb, zb), :, :, :, cols] = term.astype(jnp.bfloat16)

        each_block(body)
        core_copies[k] = start(
            tb.at[:, :, oc, :, cols], r1.at[:, :, :, cols],
            c_send.at[k], c_recv.at[k], (mz, mx, oc),
        )

    def stage_x(k):
        cols = pl.ds(k * cw, cw)
        core_copies[k].wait_recv()
        for z in range(nz):
            for x in range(nx):
                total = tf[z, x, mc, :, cols] + r1[z, x, :, cols].astype(jnp.float32)
                s1f[z, x, :, cols] = total
                s1b[z, x, :, cols] = total.astype(jnp.bfloat16)
        for d in range(1, nx):
            x = lax.rem(mx + d, nx)
            x_copies[k, d] = start(
                s1b.at[:, x, :, cols], r2.at[d - 1, :, :, cols],
                x_send.at[k, d - 1], x_recv.at[k, d - 1], (mz, x, mc),
            )

    def stage_z(k):
        cols = pl.ds(k * cw, cw)
        for d in range(1, nx):
            x_copies[k, d].wait_recv()
        for z in range(nz):
            total = s1f[z, mx, :, cols]
            for d in range(1, nx):
                total = total + r2[d - 1, z, :, cols].astype(jnp.float32)
            s2f[z, :, cols] = total
            s2b[z, :, cols] = total.astype(jnp.bfloat16)
        for d in range(1, nz):
            z = lax.rem(mz + d, nz)
            z_copies[k, d] = start(
                s2b.at[z, :, cols], r3.at[d - 1, :, cols],
                z_send.at[k, d - 1], z_recv.at[k, d - 1], (z, mx, mc),
            )

    def finish(k):
        cols = pl.ds(k * cw, cw)
        total = s2f[mz, :, cols]
        for d in range(1, nz):
            z_copies[k, d].wait_recv()
            total = total + r3[d - 1, :, cols].astype(jnp.float32)
        out_ref[:, cols] = (total * (1.0 / math.sqrt(total_recent))).astype(jnp.bfloat16)

    stages = (stage_core, stage_x, stage_z, finish)
    for step in range(CHUNKS + len(stages) - 1):
        for index, stage in enumerate(stages):
            if 0 <= step - index < CHUNKS:
                stage(step - index)
    for copy in sent + copies:
        copy.wait_send()


def per_device(dims, late_grads, projections, recent_sketches):
    nz, nx, nc = dims
    local_rows, items, kinds, width_in = late_grads.shape
    rank = projections.shape[1] // 4
    local_recent, width = recent_sketches.shape
    n = nz * nx * nc
    slab, part = local_rows * GROUP, width // GROUP
    bf16, f32 = jnp.bfloat16, jnp.float32
    dma = pltpu.SemaphoreType.DMA
    sends = (nz - 1) + nz * nx + nz * (nx - 1)
    out = pl.pallas_call(
        functools.partial(kernel, dims, items, rank, local_recent * n),
        out_shape=jax.ShapeDtypeStruct((slab, part), bf16),
        in_specs=[pl.BlockSpec(memory_space=pl.ANY)] * 3,
        out_specs=pl.BlockSpec(memory_space=pltpu.VMEM),
        scratch_shapes=[
            pltpu.VMEM((local_rows * items, kinds, width_in), bf16),
            pltpu.VMEM(projections.shape, bf16),
            pltpu.VMEM((GROUP * local_recent, part), bf16),
            pltpu.VMEM((nz, nx, nc, slab, part), bf16),
            pltpu.VMEM((n * slab, GROUP * local_recent), bf16),
            pltpu.VMEM((nz, nx, nc, slab, part), f32),
            pltpu.VMEM((nz, nx, nc, slab, part), bf16),
            pltpu.VMEM((nz, nx, slab, part), bf16),
            pltpu.VMEM((nz, nx, slab, part), f32),
            pltpu.VMEM((nz, nx, slab, part), bf16),
            pltpu.VMEM((nx - 1, nz, slab, part), bf16),
            pltpu.VMEM((nz, slab, part), f32),
            pltpu.VMEM((nz, slab, part), bf16),
            pltpu.VMEM((nz - 1, slab, part), bf16),
            dma((2 + GROUP,)),
            dma((sends + nz * nx,)),
            dma(dims),
            dma((CHUNKS,)),
            dma((CHUNKS,)),
            dma((CHUNKS, nx - 1)),
            dma((CHUNKS, nx - 1)),
            dma((CHUNKS, nz - 1)),
            dma((CHUNKS, nz - 1)),
        ],
        compiler_params=pltpu.CompilerParams(
            collective_id=0, has_side_effects=True, vmem_limit_bytes=60 * 1024 * 1024
        ),
    )(late_grads.reshape(local_rows * items, kinds, width_in), projections, recent_sketches)
    return out.reshape(local_rows, width)


def solution(mesh):
    n = mesh.shape["row"]
    nx = 4 if n >= 64 else 2
    dims = (n // (2 * nx), nx, 2)
    placed = (P(("groups", "row"), None, None, None), P(), P(("groups", "row"), None))
    return jax.shard_map(
        functools.partial(per_device, dims),
        mesh=mesh,
        in_specs=placed,
        out_specs=P(("groups", "row"), None),
        check_vma=False,
    )
```

time: 118 us -> 34.9 us (0.30)
  waiting for transfers between devices: 54.8 us -> 0 us
  blocking collectives: 34.8 us -> 0 us
  Pallas kernels: 0 us -> 33.3 us
  between operations: 13.4 us -> 0.01 us
  matrix products: 8.43 us -> 0 us
  local copies, waits for them, and re-layouts: 5.74 us -> 1.39 us
    reduce_scatter x1 -> x0, waiting for transfers between devices: 54.8 us -> none  [per_device(): col_block = lax.psum_scatter(term, 'row', scatter_dimension=1, tiled=True)]
    pallas_call x0 -> x1, Pallas kernels: none -> 33.3 us  [per_device(): pl.pallas_call(functools.partial(kernel, dims, items, rank, local_recent...]
    all_gather x1 -> x0, blocking collectives: 24.6 us -> none  [per_device(): late_all = lax.all_gather(own_sketch, 'row', axis=0, tiled=True)]
    all_to_all x1 -> x0, blocking collectives: 10.2 us -> none  [per_device(): lax.all_to_all(finished, 'row', split_axis=0, concat_axis=1, tiled=True)]
    dot_general x3 -> x0, matrix products: 7.77 us -> none  [the longest x1 7.37 us: weighted_term(): return jnp.dot(weights, recent_sketches, preferred_element_type=jnp.float32)]
    unnamed x4 -> x0, local copies, waits for them, and re-layouts: 5.53 us -> none
    reshape x2 -> x1, local copies, waits for them, and re-layouts: 0.19 us -> 1.39 us  [per_device(): return out.reshape(local_rows, width)]
  transfers between devices with their start and end apart: 1 -> 0, of which waited for: 1 -> 0; matrix products, arithmetic and copies ran while one was open for 0% -> 0% of each run, Pallas kernels for 0% -> 0%
where the time goes in v1:
time: 34.9 us; the launch traced here: 34.7 us
  Pallas kernels  33.3 us (95%)
  local copies, waits for them, and re-layouts  1.39 us (4%)
    pallas_call x1, Pallas kernels, per_device(): pl.pallas_call(functools.partial(kernel, dims, items, rank, local_recent...  33.3 us
    reshape x1, local copies, waits for them, and re-layouts, per_device(): return out.reshape(local_rows, width)  1.39 us

profile of v1, /device:TPU:0, one launch (start us, length us, event | category | flops | bytes accessed | tf_op | source)
XLA Modules:
  0.0 34.7 jit_solution(13570680579273086511)
XLA Ops:
  0.0 33.3 %shard_map.37 = bf16[16,1024]{1,0:T(8,128)(2,1)} custom-call(bf16[32,4,4096]{2,1,0:T(4,128)(2,1)} %bitcast.1, bf16[4096,256]{1,0:T(8,128)(2,1)} %proj_hbm.1, bf16[256,8192]{1,0:T(8,128)(2,1)} %recent_hbm.1), custom_call_target="tpu_custom_call" | custom-call | tf_op jit(solution)/shard_map/pallas_call | solution.py:262
  33.3 1.4 %reshape.7 = bf16[2,8192]{1,0:T(2,128)(2,1)} reshape(bf16[16,1024]{1,0:T(8,128)(2,1)} %shard_map.37) | data formatting | bytes 65536 | tf_op jit(solution)/shard_map/reshape | solution.py:296

commit v2 on v1

v2 whole, which is shorter than its diff:
```python
import functools
import math

import jax
import jax.numpy as jnp
from jax import lax
from jax.experimental import pallas as pl
from jax.experimental.pallas import tpu as pltpu
from jax.sharding import PartitionSpec as P

GROUP = 8
CHUNKS = 2
LOADS = 4
MESH = pl.DeviceIdType.MESH


def kernel(
    dims, items, rank, total_recent,
    late_hbm, proj_hbm, recent_hbm, out_ref,
    late, proj, recent, gath, wmask, tf, tb, r1, s1f, s1b, r2, s2f, s2b, r3,
    t1b, t2, t2f, t2b, t3,
    load_sem, g_send, g_recv, c_send, c_recv, x_send, x_recv, z_send, z_recv,
):
    nz, nx, nc = dims
    width = recent_hbm.shape[1]
    part = width // GROUP
    local_recent = recent_hbm.shape[0]
    slab = gath.shape[3]
    examples = slab // GROUP
    n = nz * nx * nc
    me = lax.axis_index("row")
    mc = lax.rem(me, nc)
    mx = lax.rem(lax.div(me, nc), nx)
    mz = lax.div(me, nc * nx)
    oc = 1 - mc

    def across(z, d):
        bit = 1
        while bit <= d:
            if d & bit:
                z = z + bit - 2 * bit * lax.rem(lax.div(z, bit), 2)
            bit *= 2
        return z

    def flat(z, x, c):
        return {"row": (z * nx + x) * nc + c}

    depth = late.shape[2] // LOADS
    load_inputs = []
    for i in range(LOADS):
        part_of = pl.ds(i * depth, depth)
        pair = (
            pltpu.make_async_copy(late_hbm.at[:, :, part_of], late.at[:, :, part_of], load_sem.at[GROUP + i]),
            pltpu.make_async_copy(proj_hbm.at[part_of], proj.at[part_of], load_sem.at[GROUP + LOADS + i]),
        )
        for copy in pair:
            copy.start()
        load_inputs.append(pair)

    peers = [(mz, mx, oc)]
    peers += [(mz, lax.rem(mx + d, nx), mc) for d in range(1, nx)]
    peers += [(across(mz, d), mx, mc) for d in range(1, nz)]
    barrier = pltpu.get_barrier_semaphore()
    for z, x, c in peers:
        pl.semaphore_signal(barrier, inc=1, device_id=flat(z, x, c), device_id_type=MESH)

    def onehot(shape, expr):
        r = lax.broadcasted_iota(jnp.int32, shape, 0)
        c = lax.broadcasted_iota(jnp.int32, shape, 1)
        return jnp.where(expr(r, c), 1.0, 0.0).astype(jnp.bfloat16)

    pairs = examples * items
    pick = onehot((pairs, 4 * pairs), lambda r, c: r == lax.shift_right_logical(c, 2))
    spread = onehot((rank, part), lambda r, c: r == lax.rem(c, rank))
    repeat = onehot((rank, rank * rank), lambda r, c: r == lax.div(c, rank))

    full = jnp.zeros((4 * pairs, 4 * rank), jnp.float32)
    for i, pair in enumerate(load_inputs):
        for copy in pair:
            copy.wait()
        rows = late[:, :, i * depth : (i + 1) * depth].reshape(4 * pairs, depth)
        full = full + jnp.dot(
            rows, proj[i * depth : (i + 1) * depth, :], preferred_element_type=jnp.float32
        )
    load_recent = []
    for q in range(GROUP):
        copy = pltpu.make_async_copy(
            recent_hbm.at[:, pl.ds(q * part, part)],
            recent.at[pl.ds(q * local_recent, local_recent), :],
            load_sem.at[q],
        )
        copy.start()
        load_recent.append(copy)
    kind = lax.rem(lax.broadcasted_iota(jnp.int32, full.shape, 0), 4)
    block = lax.div(lax.broadcasted_iota(jnp.int32, full.shape, 1), rank)
    full = jnp.where(kind == block, full, 0.0).astype(jnp.bfloat16)
    factors = jnp.dot(pick, full, preferred_element_type=jnp.float32)
    sketch = jnp.zeros((slab, part), jnp.float32)
    row = lax.broadcasted_iota(jnp.int32, (slab, part), 0)
    quarter = GROUP // 2
    for layer in range(2):
        right = factors[:, 2 * layer * rank : (2 * layer + 1) * rank].astype(jnp.bfloat16)
        left = factors[:, (2 * layer + 1) * rank : (2 * layer + 2) * rank].astype(jnp.bfloat16)
        tiled = jnp.dot(right, spread, preferred_element_type=jnp.float32)
        for q in range(quarter):
            wide = jnp.dot(
                left, repeat[:, q * part : (q + 1) * part], preferred_element_type=jnp.float32
            )
            outer = wide * tiled
            for e in range(examples):
                total = jnp.sum(outer[e * items : (e + 1) * items], axis=0, keepdims=True)
                at = e * GROUP + layer * quarter + q
                sketch = jnp.where(row == at, total, sketch)
    gath[mc, mx, mz] = (sketch * (1.0 / math.sqrt(items))).astype(jnp.bfloat16)

    pl.semaphore_wait(barrier, len(peers))

    sent = []

    def forward(z, x, c, to, slot):
        copy = pltpu.make_async_remote_copy(
            src_ref=gath.at[c, x, z], dst_ref=gath.at[c, x, z],
            send_sem=g_send.at[slot], recv_sem=g_recv.at[z, x, c],
            device_id=flat(*to), device_id_type=MESH,
        )
        copy.start()
        sent.append(copy)

    def arrived(z, x, c):
        pltpu.make_async_remote_copy(
            src_ref=gath.at[c, x, z], dst_ref=gath.at[c, x, z],
            send_sem=g_send.at[0], recv_sem=g_recv.at[z, x, c],
            device_id=flat(mz, mx, oc), device_id_type=MESH,
        ).wait_recv()

    slot = 0
    for d in range(1, nz):
        forward(mz, mx, mc, (across(mz, d), mx, mc), slot)
        slot += 1
    for dz in range(nz):
        z = across(mz, dz)
        if dz:
            arrived(z, mx, mc)
        for d in range(1, nx):
            forward(z, mx, mc, (mz, lax.rem(mx + d, nx), mc), slot)
            slot += 1
        forward(z, mx, mc, (mz, mx, oc), slot)
        slot += 1
    for dz in range(nz):
        z = across(mz, dz)
        for d in range(1, nx):
            x = lax.rem(mx + nx - d, nx)
            arrived(z, x, mc)
            forward(z, x, mc, (mz, mx, oc), slot)
            slot += 1
    for copy in load_recent:
        copy.wait()
    for dz in range(nz):
        z = across(mz, dz)
        for d in range(nx):
            arrived(z, lax.rem(mx + nx - d, nx), oc)

    many = min(n, 256 // slab)
    rb = many * slab
    slabs = gath.reshape(n, slab, part)

    def similar(b):
        every = slabs[pl.ds(b * many, many)].reshape(rb, part)
        group = lax.rem(lax.broadcasted_iota(jnp.int32, (rb, local_recent), 0), GROUP)
        acc = jnp.zeros((rb, local_recent), jnp.float32)
        for q in range(GROUP):
            term = lax.dot_general(
                every, recent[q * local_recent : (q + 1) * local_recent, :],
                (((1,), (1,)), ((), ())), preferred_element_type=jnp.float32,
            )
            acc = jnp.where(group == q, term, acc)
        acc = acc.reshape(rb // GROUP, GROUP, local_recent)
        sim = jnp.sum(acc, axis=1, keepdims=True) * (1.0 / math.sqrt(width))
        weights = jnp.broadcast_to(jnp.tanh(sim), acc.shape).reshape(rb, local_recent)
        for q in range(GROUP):
            wmask[pl.ds(b * rb, rb), q * local_recent : (q + 1) * local_recent] = jnp.where(
                group == q, weights, 0.0
            ).astype(jnp.bfloat16)

    def each_block(body):
        if n == many:
            body(0)
        else:
            lax.fori_loop(0, n // many, lambda b, c: (body(b), c)[1], 0)

    each_block(similar)

    cw = part // CHUNKS
    copies = []

    def start(src, dst, ss, rs, to):
        copy = pltpu.make_async_remote_copy(
            src_ref=src, dst_ref=dst, send_sem=ss, recv_sem=rs,
            device_id=flat(*to), device_id_type=MESH,
        )
        copy.start()
        copies.append(copy)
        return copy

    core_copies, x_copies, z_copies = {}, {}, {}

    def stage_core(k):
        def body(b):
            term = jnp.dot(
                wmask[pl.ds(b * rb, rb), :], recent[:, k * cw : (k + 1) * cw],
                preferred_element_type=jnp.float32,
            ).reshape(many, slab, cw)
            tf.at[k].reshape(n, slab, cw)[pl.ds(b * many, many)] = term
            tb.at[k].reshape(n, slab, cw)[pl.ds(b * many, many)] = term.astype(jnp.bfloat16)

        each_block(body)
        core_copies[k] = start(
            tb.at[k, oc], r1.at[k], c_send.at[k], c_recv.at[k], (mz, mx, oc)
        )

    def send_x(k, src, dst):
        for d in range(1, nx):
            x = lax.rem(mx + d, nx)
            x_copies[k, d] = start(
                src.at[k, x], dst.at[k, d - 1],
                x_send.at[k, d - 1], x_recv.at[k, d - 1], (mz, x, mc),
            )

    def send_z(k, src, dst):
        for d in reversed(range(1, nz)):
            z = across(mz, d)
            z_copies[k, d] = start(
                src.at[k, z], dst.at[k, d - 1],
                z_send.at[k, d - 1], z_recv.at[k, d - 1], (z, mx, mc),
            )

    def add(total, copies, k, source):
        for d in range(1, source.shape[1] + 1):
            copies[k, d].wait_recv()
            total = total + source[k, d - 1].astype(jnp.float32)
        return total

    def stage_first(k):
        core_copies[k].wait_recv()
        total = tf[k, mc] + r1[k].astype(jnp.float32)
        if k % 2:
            s1f[k] = total
            for z in range(nz):
                t1b[k // 2, z] = total[:, z].astype(jnp.bfloat16)
            for d in reversed(range(1, nz)):
                z = across(mz, d)
                z_copies[k, d] = start(
                    t1b.at[k // 2, z], t2.at[k // 2, d - 1],
                    z_send.at[k, d - 1], z_recv.at[k, d - 1], (z, mx, mc),
                )
        else:
            s1f[k] = total
            s1b[k] = total.astype(jnp.bfloat16)
            send_x(k, s1b, r2)

    def stage_second(k):
        if k % 2:
            total = s1f[k, :, mz]
            for d in range(1, nz):
                z_copies[k, d].wait_recv()
                total = total + t2[k // 2, d - 1].astype(jnp.float32)
            t2f[k // 2] = total
            t2b[k // 2] = total.astype(jnp.bfloat16)
            for d in range(1, nx):
                x = lax.rem(mx + d, nx)
                x_copies[k, d] = start(
                    t2b.at[k // 2, x], t3.at[k // 2, d - 1],
                    x_send.at[k, d - 1], x_recv.at[k, d - 1], (mz, x, mc),
                )
        else:
            total = add(s1f[k, mx], x_copies, k, r2)
            s2f[k] = total
            s2b[k] = total.astype(jnp.bfloat16)
            send_z(k, s2b, r3)

    def finish(k):
        if k % 2:
            total = t2f[k // 2, mx]
            for d in range(1, nx):
                x_copies[k, d].wait_recv()
                total = total + t3[k // 2, d - 1].astype(jnp.float32)
        else:
            total = add(s2f[k, mz], z_copies, k, r3)
        out_ref[:, k * cw : (k + 1) * cw] = (
            total * (1.0 / math.sqrt(total_recent))
        ).astype(jnp.bfloat16)

    stages = (stage_core, stage_first, stage_second, finish)
    for stage in stages:
        for k in range(CHUNKS):
            stage(k)
    for copy in sent + copies:
        copy.wait_send()


def per_device(dims, late_grads, projections, recent_sketches):
    nz, nx, nc = dims
    local_rows, items, kinds, width_in = late_grads.shape
    rank = projections.shape[1] // 4
    local_recent, width = recent_sketches.shape
    n = nz * nx * nc
    slab, part = local_rows * GROUP, width // GROUP
    bf16, f32 = jnp.bfloat16, jnp.float32
    dma = pltpu.SemaphoreType.DMA
    cw = part // CHUNKS
    sends = (nz - 1) + nz * nx + nz * (nx - 1)
    out = pl.pallas_call(
        functools.partial(kernel, dims, items, rank, local_recent * n),
        out_shape=pltpu.VMEM((slab, part), bf16),
        in_specs=[pl.BlockSpec(memory_space=pl.ANY)] * 3,
        out_specs=pl.BlockSpec(memory_space=pltpu.VMEM),
        scratch_shapes=[
            pltpu.VMEM((local_rows * items, kinds, width_in), bf16),
            pltpu.VMEM(projections.shape, bf16),
            pltpu.VMEM((GROUP * local_recent, part), bf16),
            pltpu.VMEM((nc, nx, nz, slab, part), bf16),
            pltpu.VMEM((n * slab, GROUP * local_recent), bf16),
            pltpu.VMEM((CHUNKS, nc, nx, nz, slab, cw), f32),
            pltpu.VMEM((CHUNKS, nc, nx, nz, slab, cw), bf16),
            pltpu.VMEM((CHUNKS, nx, nz, slab, cw), bf16),
            pltpu.VMEM((CHUNKS, nx, nz, slab, cw), f32),
            pltpu.VMEM((CHUNKS, nx, nz, slab, cw), bf16),
            pltpu.VMEM((CHUNKS, nx - 1, nz, slab, cw), bf16),
            pltpu.VMEM((CHUNKS, nz, slab, cw), f32),
            pltpu.VMEM((CHUNKS, nz, slab, cw), bf16),
            pltpu.VMEM((CHUNKS, nz - 1, slab, cw), bf16),
            pltpu.VMEM((CHUNKS // 2, nz, nx, slab, cw), bf16),
            pltpu.VMEM((CHUNKS // 2, nz - 1, nx, slab, cw), bf16),
            pltpu.VMEM((CHUNKS // 2, nx, slab, cw), f32),
            pltpu.VMEM((CHUNKS // 2, nx, slab, cw), bf16),
            pltpu.VMEM((CHUNKS // 2, nx - 1, slab, cw), bf16),
            dma((GROUP + 2 * LOADS,)),
            dma((sends + nz * nx,)),
            dma(dims),
            dma((CHUNKS,)),
            dma((CHUNKS,)),
            dma((CHUNKS, nx - 1)),
            dma((CHUNKS, nx - 1)),
            dma((CHUNKS, nz - 1)),
            dma((CHUNKS, nz - 1)),
        ],
        compiler_params=pltpu.CompilerParams(
            collective_id=0, has_side_effects=True, vmem_limit_bytes=60 * 1024 * 1024
        ),
    )(late_grads.reshape(local_rows * items, kinds, width_in), projections, recent_sketches)
    return out.reshape(local_rows, width)


def solution(mesh):
    n = mesh.shape["row"]
    nx = 4 if n >= 64 else 2
    dims = (n // (2 * nx), nx, 2)
    placed = (P(("groups", "row"), None, None, None), P(), P(("groups", "row"), None))
    return jax.shard_map(
        functools.partial(per_device, dims),
        mesh=mesh,
        in_specs=placed,
        out_specs=P(("groups", "row"), None),
        check_vma=False,
    )
```

time: 34.9 us -> 26.2 us (0.75)
  Pallas kernels: 33.3 us -> 25.4 us
  local copies, waits for them, and re-layouts: 1.39 us -> 0.63 us
    pallas_call x1, Pallas kernels: 33.3 us -> 25.4 us  [per_device(): pl.pallas_call(functools.partial(kernel, dims, items, rank, local_recent...]
    reshape x1, local copies, waits for them, and re-layouts: 1.39 us -> 0.63 us  [per_device(): return out.reshape(local_rows, width)]
where the time goes in v2:
time: 26.2 us; the launch traced here: 26 us
  Pallas kernels  25.4 us (97%)
  local copies, waits for them, and re-layouts  0.63 us (2%)
    pallas_call x1, Pallas kernels, per_device(): pl.pallas_call(functools.partial(kernel, dims, items, rank, local_recent...  25.4 us
    reshape x1, local copies, waits for them, and re-layouts, per_device(): return out.reshape(local_rows, width)  0.63 us

profile of v2, /device:TPU:0, one launch (start us, length us, event | category | flops | bytes accessed | tf_op | source)
XLA Modules:
  0.0 26.0 jit_solution(9574038652484534654)
XLA Ops:
  0.0 25.4 %shard_map.37 = bf16[16,1024]{1,0:T(8,128)(2,1)S(1)} custom-call(bf16[32,4,4096]{2,1,0:T(4,128)(2,1)} %bitcast.1, bf16[4096,256]{1,0:T(8,128)(2,1)} %proj_hbm.1, bf16[256,8192]{1,0:T(8,128)(2,1)} %recent_hbm.1), custom_call_target="tpu_custom_call" | custom-call | tf_op jit(solution)/shard_map/pallas_call | solution.py:312
  25.4 0.6 %reshape.7 = bf16[2,8192]{1,0:T(2,128)(2,1)} reshape(bf16[16,1024]{1,0:T(8,128)(2,1)S(1)} %shard_map.37) | data formatting | bytes 65536 | tf_op jit(solution)/shard_map/reshape | solution.py:351

commit v3 on v2

--- a/solution.py
+++ b/solution.py
@@ -57,6 +57,16 @@
             copy.start()
         load_inputs.append(pair)
 
+    load_recent = []
+    for q in range(GROUP):
+        copy = pltpu.make_async_copy(
+            recent_hbm.at[:, pl.ds(q * part, part)],
+            recent.at[pl.ds(q * local_recent, local_recent), :],
+            load_sem.at[q],
+        )
+        copy.start()
+        load_recent.append(copy)
+
     peers = [(mz, mx, oc)]
     peers += [(mz, lax.rem(mx + d, nx), mc) for d in range(1, nx)]
     peers += [(across(mz, d), mx, mc) for d in range(1, nz)]
@@ -82,15 +92,6 @@
         full = full + jnp.dot(
             rows, proj[i * depth : (i + 1) * depth, :], preferred_element_type=jnp.float32
         )
-    load_recent = []
-    for q in range(GROUP):
-        copy = pltpu.make_async_copy(
-            recent_hbm.at[:, pl.ds(q * part, part)],
-            recent.at[pl.ds(q * local_recent, local_recent), :],
-            load_sem.at[q],
-        )
-        copy.start()
-        load_recent.append(copy)
     kind = lax.rem(lax.broadcasted_iota(jnp.int32, full.shape, 0), 4)
     block = lax.div(lax.broadcasted_iota(jnp.int32, full.shape, 1), rank)
     full = jnp.where(kind == block, full, 0.0).astype(jnp.bfloat16)

time: 26.2 us -> 26.2 us (level)
  no operation moved by 1% of the time
where the time goes in v3:
time: 26.2 us; the launch traced here: 26 us
  Pallas kernels  25.4 us (97%)
  local copies, waits for them, and re-layouts  0.63 us (2%)
    pallas_call x1, Pallas kernels, per_device(): pl.pallas_call(functools.partial(kernel, dims, items, rank, local_recent...  25.4 us
    reshape x1, local copies, waits for them, and re-layouts, per_device(): return out.reshape(local_rows, width)  0.63 us

profile of v3, /device:TPU:0, one launch (start us, length us, event | category | flops | bytes accessed | tf_op | source)
XLA Modules:
  0.0 26.0 jit_solution(1985777019105827146)
XLA Ops:
  0.0 25.4 %shard_map.37 = bf16[16,1024]{1,0:T(8,128)(2,1)S(1)} custom-call(bf16[32,4,4096]{2,1,0:T(4,128)(2,1)} %bitcast.1, bf16[4096,256]{1,0:T(8,128)(2,1)} %proj_hbm.1, bf16[256,8192]{1,0:T(8,128)(2,1)} %recent_hbm.1), custom_call_target="tpu_custom_call" | custom-call | tf_op jit(solution)/shard_map/pallas_call | solution.py:313
  25.4 0.6 %reshape.7 = bf16[2,8192]{1,0:T(2,128)(2,1)} reshape(bf16[16,1024]{1,0:T(8,128)(2,1)S(1)} %shard_map.37) | data formatting | bytes 65536 | tf_op jit(solution)/shard_map/reshape | solution.py:352
